TPU v7x, 32 devices: a whole 2x2x4 slice. The times are simulated.
32 devices in a mesh: frame: 16 (over z, y, x), row: 2 (over core).
Axes of the slice: x: 2, y: 2, z: 4, core: 2. Of those that a mesh axis runs over, the one named last changes fastest.
Arguments:
- tokens: bfloat16 [16, 2, 128, 2048], P('frame', 'row'), may hold values from -6 to 6
- cotangent: bfloat16 [16, 2, 128, 2048], P('frame', 'row'), may hold values from -6 to 6
- timestep: int32 [1], replicated, may hold values from 0 to 999
- mod_weight: bfloat16 [256, 4096], P(None, 'frame'), may hold values from -0.375 to 0.375
- proj_weight: bfloat16 [2048, 256], P('frame'), may hold values from -0.125 to 0.125
- step_weight: bfloat16 [2048, 32], P('frame'), may hold values from -0.125 to 0.125
- step_bias: float32 [32], replicated, may hold values from -1 to 1
- rate_space: float32 [32], replicated, may hold values from 0.001171875 to 0.05
- rate_time: float32 [32], replicated, may hold values from 0.01875 to 1
- skip_gain: float32 [32], replicated, may hold values from 0.5 to 1.5
Outputs:
- mixed: bfloat16 [16, 2, 128, 2048], P('frame', 'row')
- d_tokens: bfloat16 [16, 2, 128, 2048], P('frame', 'row')
- grad_proj: float32 [2048, 256], P('frame')
- grad_step: float32 [2048, 32], P('frame')
- grad_mod: float32 [256, 4096], P(None, 'frame')
All inputs are finite; a program needn't handle non-finite values.
Results may differ from a plain program's by a relative error of at most 0.015.
Values may be sent and summed in bfloat16 or wider, within the bound.
No kernel may reach another device: no remote copies, remote signals or barrier semaphores. Data moves between devices by JAX's collectives and lax.ppermute only.
A program may use at most 64 MiB of HBM per device.

v0:
```python
import math
import jax
import jax.numpy as jnp
from jax import lax
from jax.sharding import PartitionSpec as P

norm_eps = 1e-05


def prefix(array, axis, join, neutral):
    place = lax.axis_index(axis)
    gathered = jax.tree.map(
        lambda a, kind: lax.all_gather(a.astype(kind), axis), array, (jnp.bfloat16, jnp.bfloat16)
    )
    state = jax.tree.map(lambda a, e: jnp.zeros_like(a) + jnp.asarray(e, a.dtype), array, neutral)

    def prefix_one(hop, state):
        return join(
            state,
            jax.tree.map(
                lambda a, own: lax.dynamic_index_in_dim(a, hop, 0, False).astype(own.dtype),
                gathered,
                array,
            ),
        )

    return lax.fori_loop(0, place, prefix_one, state)


def carried_in(array, axis, join, neutral):
    count = lax.axis_size(axis)
    place = lax.axis_index(axis)
    ahead = count - 1 - place
    gathered = jax.tree.map(
        lambda a, kind: lax.all_gather(a.astype(kind), axis),
        array,
        jax.tree.map(lambda a: jnp.bfloat16 if a.dtype == jnp.float32 else a.dtype, array),
    )
    state = jax.tree.map(lambda a, e: jnp.zeros_like(a) + jnp.asarray(e, a.dtype), array, neutral)

    def carried_one(hop, state):
        source = count - 1 - hop
        return join(
            state,
            jax.tree.map(
                lambda a, own: lax.dynamic_index_in_dim(a, source, 0, False).astype(own.dtype),
                gathered,
                array,
            ),
        )

    return lax.fori_loop(0, ahead, carried_one, state)


def time_embed(timestep, embed_dim):
    half_dim = embed_dim // 2
    frequency = jnp.exp(-math.log(10000.0) * jnp.arange(half_dim, dtype=jnp.float32) / half_dim)
    angles = timestep.astype(jnp.float32)[:, None] * frequency[None, :]
    return jax.nn.silu(jnp.concatenate([jnp.cos(angles), jnp.sin(angles)], axis=1))


def normalize(values):
    return values * lax.rsqrt(jnp.mean(values * values, axis=-1, keepdims=True) + norm_eps)


def block_parts(normed, coeffs, logits, step_bias, decay_rate, need_end):
    seq_count, length, feat_width = normed.shape
    head_count = decay_rate.shape[0]
    inputs = normed.reshape(seq_count, length, head_count, feat_width // head_count)
    state_size = coeffs.shape[-1] // 2
    b_part = coeffs[..., :state_size]
    c_part = coeffs[..., state_size:]
    step_size = jax.nn.softplus(logits.astype(jnp.float32) + step_bias)
    cum_log = jnp.cumsum(-step_size * decay_rate, axis=1)
    scores = (
        jnp.einsum("stn,sun->stu", c_part, b_part, preferred_element_type=jnp.float32) / state_size
    )
    lag_rows = jnp.swapaxes(cum_log, 1, 2)
    causal = jnp.tril(jnp.ones((length, length), dtype=bool))
    differences = lag_rows[:, :, :, None] - lag_rows[:, :, None, :]
    decays = jnp.where(causal, jnp.exp(jnp.where(causal, differences, 0.0)), 0.0)
    spread = jnp.swapaxes(step_size, 1, 2)
    weights = (scores[:, None, :, :] * decays * spread[:, :, None, :]).astype(jnp.bfloat16)
    inner_out = jnp.einsum("shtu,suhp->sthp", weights, inputs, preferred_element_type=jnp.float32)
    inner_out = inner_out.reshape(seq_count, length, feat_width)
    if need_end:
        end_log = cum_log[:, -1:, :]
        lead_decay = jnp.exp(end_log - cum_log) * step_size
        scaled = (inputs.astype(jnp.float32) * lead_decay[..., None]).astype(jnp.bfloat16)
        end_local = jnp.einsum("sthp,stn->shpn", scaled, b_part, preferred_element_type=jnp.float32)
    else:
        end_local = jnp.zeros(
            (seq_count, head_count, feat_width // head_count, state_size), jnp.float32
        )
    return (inner_out, end_local, cum_log, c_part)


def carry_term(cum_log, c_part, state_in):
    seq_count, length, head_count = cum_log.shape
    state_size = c_part.shape[-1]
    reached = jnp.einsum(
        "stn,shpn->sthp", c_part.astype(jnp.float32), state_in, precision=lax.Precision.HIGHEST
    )
    return (reached * jnp.exp(cum_log)[..., None] / state_size).reshape(seq_count, length, -1)


def combine_forward(earlier, later):
    return (earlier[0] * later[0], later[0][:, :, None, None] * earlier[1] + later[1])


def combine_backward(earlier, later):
    return (earlier[0] * later[0], later[1] + later[0][:, :, None, None] * earlier[1])


def per_device(
    tokens,
    cotangent,
    timestep,
    mod_weight,
    proj_weight,
    step_weight,
    step_bias,
    rate_space,
    rate_time,
    skip_gain,
):
    frame_count = lax.axis_size("frame")
    row_count = lax.axis_size("row")
    frame_id = lax.axis_index("frame")
    feat_width = tokens.shape[-1]
    band_len = tokens.shape[1] * tokens.shape[2]
    clip_count = timestep.shape[0]
    clip_frames = frame_count // clip_count
    site_count = band_len // frame_count
    head_count = rate_space.shape[0]
    clip_id = frame_id // clip_frames
    factor = (frame_count * row_count * band_len) ** (-0.5)
    activated = time_embed(timestep, mod_weight.shape[0]).astype(jnp.bfloat16)
    proj_full, step_full = (
        lax.all_gather(proj_weight, "frame", axis=0, tiled=True),
        lax.all_gather(step_weight, "frame", axis=0, tiled=True),
    )
    mod_full = lax.all_gather(mod_weight, "frame", axis=1, tiled=True)
    modulation = jnp.dot(activated, mod_full, preferred_element_type=jnp.float32)
    clip_mod = lax.dynamic_index_in_dim(modulation, clip_id, 0, keepdims=False)
    shift_vec = clip_mod[:feat_width]
    scale_vec = clip_mod[feat_width:]
    tokens_wide = tokens.reshape(band_len, feat_width).astype(jnp.float32)
    unit_rows = normalize(tokens_wide)
    normed = (unit_rows * (1.0 + scale_vec) + shift_vec).astype(jnp.bfloat16)
    projected = jnp.dot(normed, proj_full, preferred_element_type=jnp.float32).astype(jnp.bfloat16)
    logits = jnp.dot(normed, step_full, preferred_element_type=jnp.float32).astype(jnp.bfloat16)
    skip_full = jnp.repeat(skip_gain, feat_width // head_count)
    flat_grad = cotangent.reshape(band_len, feat_width)

    def space_parts(normed_band, proj_band, logit_band):
        return block_parts(normed_band, proj_band, logit_band, step_bias, rate_space, True)

    parts_out, parts_pull = jax.vjp(space_parts, normed[None], projected[None], logits[None])
    inner_out, end_local, cum_log, c_part = parts_out
    end_decay = jnp.exp(cum_log[:, -1, :])
    identity = (jnp.ones_like(end_decay), jnp.zeros_like(end_local))
    prefix_decay, state_in = prefix((end_decay, end_local), "row", combine_forward, identity)
    carried, carry_pull = jax.vjp(carry_term, cum_log, c_part, state_in)
    space_out = (inner_out + carried)[0]
    site_normed, site_grad = (
        lax.all_to_all(normed, "frame", split_axis=0, concat_axis=0, tiled=True),
        lax.all_to_all(flat_grad, "frame", split_axis=0, concat_axis=0, tiled=True),
    )
    site_proj = jnp.dot(site_normed, proj_full, preferred_element_type=jnp.float32).astype(
        jnp.bfloat16
    )
    site_logits = jnp.dot(site_normed, step_full, preferred_element_type=jnp.float32).astype(
        jnp.bfloat16
    )

    def to_seq(member):
        shaped = member.reshape(frame_count, site_count, member.shape[-1])
        return shaped.transpose(1, 0, 2)

    def from_seq(member):
        return member.transpose(1, 0, 2).reshape(frame_count * site_count, member.shape[-1])

    def time_path(normed_seq, proj_seq, logit_seq):
        return block_parts(normed_seq, proj_seq, logit_seq, step_bias, rate_time, False)[0]

    time_out, time_pull = jax.vjp(
        time_path, to_seq(site_normed), to_seq(site_proj), to_seq(site_logits)
    )
    time_low = from_seq(time_out.astype(jnp.bfloat16))
    time_dnorm, time_dproj, time_dlogit = time_pull(to_seq(site_grad).astype(jnp.float32))
    site_dproj = from_seq(time_dproj)
    site_dlogit = from_seq(time_dlogit)
    site_back = (
        from_seq(time_dnorm).astype(jnp.float32)
        + jnp.dot(site_dproj, proj_full.T, preferred_element_type=jnp.float32)
        + jnp.dot(site_dlogit, step_full.T, preferred_element_type=jnp.float32)
    ).astype(jnp.bfloat16)
    proj_time = jnp.dot(site_normed.T, site_dproj, preferred_element_type=jnp.float32)
    step_time = jnp.dot(site_normed.T, site_dlogit, preferred_element_type=jnp.float32)
    space_time, time_back = (
        lax.all_to_all(time_low, "frame", split_axis=0, concat_axis=0, tiled=True),
        lax.all_to_all(site_back, "frame", split_axis=0, concat_axis=0, tiled=True),
    )
    mixed = (
        space_out + space_time.astype(jnp.float32) + skip_full * normed.astype(jnp.float32)
    ).astype(jnp.bfloat16)
    upstream = flat_grad.astype(jnp.float32)
    carry_dcum, carry_dc, own_state = carry_pull(upstream[None])
    suffix_decay, later_grad = carried_in((end_decay, own_state), "row", combine_backward, identity)
    end_dlog = jnp.sum(later_grad * state_in, axis=(2, 3)) * end_decay
    carry_dcum = carry_dcum.at[:, -1, :].add(end_dlog)
    space_dnorm, space_dproj, space_dlogit = parts_pull(
        (upstream[None], later_grad, carry_dcum, carry_dc)
    )
    skip_dnorm = (upstream * skip_full).astype(jnp.bfloat16)
    total_dnorm = space_dnorm[0] + skip_dnorm
    pre_grad = (
        total_dnorm.astype(jnp.float32)
        + jnp.dot(space_dproj[0], proj_full.T, preferred_element_type=jnp.float32)
        + jnp.dot(space_dlogit[0], step_full.T, preferred_element_type=jnp.float32)
        + time_back.astype(jnp.float32)
    )
    proj_term = jnp.dot(normed.T, space_dproj[0], preferred_element_type=jnp.float32) + proj_time
    step_term = jnp.dot(normed.T, space_dlogit[0], preferred_element_type=jnp.float32) + step_time
    shift_grad = jnp.sum(pre_grad, axis=0)
    scale_grad = jnp.sum(pre_grad * unit_rows, axis=0)
    picked = (jnp.arange(clip_count) == clip_id).astype(jnp.float32)
    mod_term = jnp.concatenate([shift_grad, scale_grad])[:, None] * picked[None, :]
    proj_sum, step_sum, mod_sum = (
        lax.psum(proj_term.astype(jnp.bfloat16), "row").astype(jnp.float32),
        lax.psum(step_term.astype(jnp.bfloat16), "row").astype(jnp.float32),
        lax.psum(mod_term.astype(jnp.bfloat16), "row").astype(jnp.float32),
    )
    proj_sum, step_sum, mod_sum = (
        lax.psum_scatter(proj_sum, "frame", scatter_dimension=0, tiled=True),
        lax.psum_scatter(step_sum, "frame", scatter_dimension=0, tiled=True),
        lax.psum_scatter(mod_sum, "frame", scatter_dimension=0, tiled=True),
    )
    grad_proj = proj_sum * factor
    grad_step = step_sum * factor
    grad_mod = (
        jnp.dot(activated.astype(jnp.float32).T, mod_sum.T, precision=lax.Precision.HIGHEST)
        * factor
    )
    unused, norm_pull = jax.vjp(normalize, tokens_wide)
    (tokens_grad,) = norm_pull(pre_grad * (1.0 + scale_vec))
    d_tokens = tokens_grad.astype(jnp.bfloat16).reshape(tokens.shape)
    return (mixed.reshape(tokens.shape), d_tokens, grad_proj, grad_step, grad_mod)


def solution(mesh):
    placed = (
        P("frame", "row", None, None),
        P("frame", "row", None, None),
        P(),
        P(None, "frame"),
        P("frame", None),
        P("frame", None),
        P(),
        P(),
        P(),
        P(),
    )
    return jax.shard_map(
        per_device,
        mesh=mesh,
        in_specs=placed,
        out_specs=(
            P("frame", "row", None, None),
            P("frame", "row", None, None),
            P("frame", None),
            P("frame", None),
            P(None, "frame"),
        ),
        check_vma=False,
    )
```

profile of v0, /device:TPU:0, one launch (start us, length us, event | category | flops | bytes accessed | tf_op | source)
XLA Modules:
  0.0 490.7 jit_solution(3879071118985589353)
XLA Ops:
  7.9 8.4 %all-to-all-start.2 = ((bf16[16,8,2048]{2,1,0:T(8,128)(2,1)}), bf16[16,8,2048]{2,1,0:T(8,128)(2,1)S(1)}, u32[]{:S(2)}, u32[]{:S(2)}) async-start(bf16[16,8,2048]{2,1,0:T(8,128)(2,1)} %bitcast.449), calls=%async_computation.2 | async-start | bytes 1048576 | tf_op jit(solution)/shard_map/all_to_all | solution.py:168
  17.0 2.0 copy.217
  22.7 42.0 %all_gather.29 = bf16[2048,32]{0,1:T(8,128)(2,1)S(1)} all-gather(bf16[128,32]{0,1:T(8,128)(2,1)S(1)} %copy-done.52), channel_id=1, replica_groups=mesh['frame'=16,'row'=2] {'frame'}, dimensions={0}, use_global_device_ids=true | all-gather | bytes 139264 | tf_op jit(solution)/shard_map/all_gather | solution.py:141
  65.8 2.1 reshape.933
  67.9 12.4 %all-gather.7.cloned.1.call-done = bf16[256,4096]{1,0:T(8,128)(2,1)} async-done(((bf16[256,256]{1,0:T(8,128)(2,1)}), bf16[256,4096]{1,0:T(8,128)(2,1)}) %all-gather.7.cloned.1.call-update) | async-done | bytes 2097168 | tf_op jit(solution)/shard_map/all_gather | solution.py:143
  80.3 2.0 fusion.182
  85.5 4.0 all-to-all-start
  89.5 2.5 convert_multiply_fusion
  93.3 1.5 copy.214
  94.9 42.8 %all-gather.9.cloned.1.call-done = bf16[2048,256]{1,0:T(8,128)(2,1)} async-done(((bf16[128,256]{1,0:T(8,128)(2,1)}), bf16[2048,256]{1,0:T(8,128)(2,1)}) %all-gather.9.cloned.1.call-update) | async-done | bytes 1048592 | tf_op jit(solution)/shard_map/all_gather | solution.py:140
  137.7 1.6 fusion.33
  139.3 1.4 convolution_convert_fusion.5
  141.2 2.1 all_gather.30
  151.7 3.2 convert_bitcast_fusion
  155.0 3.5 fusion.26
  160.1 2.0 copy.231
  162.0 2.1 reshape.922
  164.1 1.6 copy.237
  165.7 1.6 copy.236
  172.1 4.5 all-to-all-start.3
  176.8 1.4 while.28
  178.3 2.1 multiply_reduce_fusion.2
  181.2 1.9 fusion.177
  184.3 1.6 copy.197
  185.8 1.7 fusion.50
  190.0 2.7 convolution_bitcast_fusion
  195.5 3.8 fusion.24
  204.2 2.4 fusion.35
  206.6 2.2 multiply_reduce_fusion.1
  213.5 2.0 fusion.4
  215.7 2.4 fusion
  218.2 2.3 fusion.32
  221.6 1.5 convolution_add_fusion.4
  223.1 2.6 fusion.70
  225.8 4.2 psum.23
  230.0 1.8 copy.246
  231.8 7.7 %all-reduce.8.cloned.1.call-done = (bf16[2048,256]{1,0:T(8,128)(2,1)}, bf16[2048,32]{0,1:T(8,128)(2,1)}) async-done(((bf16[2048,256]{1,0:T(8,128)(2,1)}, bf16[2048,32]{0,1:T(8,128)(2,1)}), (bf16[2048,256]{1,0:T(8,128)(2,1)}, bf16[2048,32]{0,1:T(8,128)(2,1)})) %all-reduce.8.cloned.1.call-update) | async-done | bytes 1179664 | tf_op jit(solution)/shard_map/psum | solution.py:231
  239.5 1.6 convert_element_type.535
  241.3 2.8 convert_element_type.533
  247.7 6.8 %all-to-all-start.1 = ((bf16[16,8,2048]{2,1,0:T(8,128)(2,1)}), bf16[16,8,2048]{2,1,0:T(8,128)(2,1)S(1)}, u32[]{:S(2)}, u32[]{:S(2)}) async-start(bf16[16,8,2048]{2,1,0:T(8,128)(2,1)} %copy.211), calls=%async_computation.1 | async-start | bytes 1048576 | tf_op jit(solution)/shard_map/all_to_all | solution.py:202
  254.6 2.8 fusion.80
  257.4 2.7 copy.201
  262.6 10.8 %all-to-all-done.1 = bf16[16,8,2048]{2,1,0:T(8,128)(2,1)S(1)} async-done(((bf16[16,8,2048]{2,1,0:T(8,128)(2,1)}), bf16[16,8,2048]{2,1,0:T(8,128)(2,1)S(1)}, u32[]{:S(2)}, u32[]{:S(2)}) %all-to-all-start.1) | async-done | bytes 524320 | tf_op jit(solution)/shard_map/all_to_all | solution.py:202
  273.4 2.4 fusion.52
  275.8 50.2 %reduce-scatter.10.cloned.1.call-done = f32[256,1]{1,0:T(8,128)} async-done(((f32[4096,1]{1,0:T(8,128)}), f32[256,1]{1,0:T(8,128)}) %reduce-scatter.10.cloned.1.call-update) | async-done | bytes 1040
  327.7 74.5 %reduce-scatter.8.cloned.1.call-done = f32[128,32]{0,1:T(8,128)} async-done(((f32[2048,32]{0,1:T(8,128)}), f32[128,32]{0,1:T(8,128)}) %reduce-scatter.8.cloned.1.call-update) | async-done | bytes 16400 | tf_op jit(solution)/shard_map/reduce_scatter | solution.py:237
  403.6 78.7 %reduce-scatter.6.cloned.1.call-done = f32[128,256]{1,0:T(8,128)} async-done(((f32[2048,256]{1,0:T(8,128)}), f32[128,256]{1,0:T(8,128)}) %reduce-scatter.6.cloned.1.call-update) | async-done | bytes 131088 | tf_op jit(solution)/shard_map/reduce_scatter | solution.py:236
  482.3 1.6 broadcast_multiply_fusion
  (229 shorter events, 53.7 us)
Async XLA Ops:
  7.2 13.2 %copy-start = (bf16[1,1,128,2048]{3,2,1,0:T(8,128)(2,1)S(1)}, bf16[1,1,128,2048]{3,2,1,0:T(8,128)(2,1)}, u32[]{:S(2)}) copy-start(bf16[1,1,128,2048]{3,2,1,0:T(8,128)(2,1)} %param.16) | copy-start | bytes 1572868
  7.2 14.5 %copy-start.60 = (f32[32]{0:T(128)S(1)}, f32[32]{0:T(128)}, u32[]{:S(2)}) copy-start(f32[32]{0:T(128)} %param.25) | copy-start | bytes 388
  7.2 73.2 %all-gather.7.cloned.1.call-start = ((), (), s32[]{:S(2)}) async-start(), calls=%async_computation.7 | async-start | bytes 2228224 | tf_op jit(solution)/shard_map/all_gather | solution.py:143
  7.9 14.8 %copy-start.52 = (bf16[128,32]{0,1:T(8,128)(2,1)S(1)}, bf16[128,32]{0,1:T(8,128)(2,1)}, u32[]{:S(2)}) copy-start(bf16[128,32]{0,1:T(8,128)(2,1)} %param.21) | copy-start | bytes 24580
  7.9 57.9 %all-to-all-start.2 = ((bf16[16,8,2048]{2,1,0:T(8,128)(2,1)}), bf16[16,8,2048]{2,1,0:T(8,128)(2,1)S(1)}, u32[]{:S(2)}, u32[]{:S(2)}) async-start(bf16[16,8,2048]{2,1,0:T(8,128)(2,1)} %bitcast.449), calls=%async_computation.2 | async-start | bytes 1048576 | tf_op jit(solution)/shard_map/all_to_all | solution.py:168
  16.3 121.4 %all-gather.9.cloned.1.call-start = ((), (), s32[]{:S(2)}) async-start(), calls=%async_computation.8 | async-start | bytes 1114112 | tf_op jit(solution)/shard_map/all_gather | solution.py:140
  22.4 59.9 %copy-start.53 = (f32[32]{0:T(128)S(1)}, f32[32]{0:T(128)}, u32[]{:S(2)}) copy-start(f32[32]{0:T(128)} %param.22) | copy-start | bytes 388
  22.6 60.1 %copy-start.58 = (f32[128]{0:T(128)}, f32[128]{0:T(128)S(1)}, u32[]{:S(2)}) copy-start(f32[128]{0:T(128)S(1)} %fusion.74) | copy-start | bytes 1540
  22.6 115.1 %copy-start.45 = (f32[128]{0:T(128)}, f32[128]{0:T(128)S(1)}, u32[]{:S(2)}) copy-start(f32[128]{0:T(128)S(1)} %fusion.158) | copy-start | bytes 1540
  67.9 14.8 %copy-start.55 = (f32[32]{0:T(128)S(1)}, f32[32]{0:T(128)}, u32[]{:S(2)}) copy-start(f32[32]{0:T(128)} %param.23) | copy-start | bytes 388
  83.1 6.4 %copy-start.5 = (bf16[1,1,128,2048]{3,2,1,0:T(8,128)(2,1)S(1)}, bf16[1,1,128,2048]{3,2,1,0:T(8,128)(2,1)}, u32[]{:S(2)}) copy-start(bf16[1,1,128,2048]{3,2,1,0:T(8,128)(2,1)} %param.17) | copy-start | bytes 1572868
  85.5 60.6 %all-to-all-start = ((bf16[16,8,2048]{2,1,0:T(8,128)(2,1)}), bf16[16,8,2048]{2,1,0:T(8,128)(2,1)S(1)}, u32[]{:S(2)}, u32[]{:S(2)}) async-start(bf16[16,8,2048]{2,1,0:T(8,128)(2,1)} %fusion.62), calls=%async_computation | async-start | bytes 1048576 | tf_op jit(solution)/shard_map/all_to_all | solution.py:167
  89.5 87.2 %all-gather.13.cloned.1.call-start = ((), (), s32[]{:S(2)}) async-start(), calls=%async_computation.12 | async-start | bytes 1572864 | tf_op jit(solution)/shard_map/all_gather | solution.py:35
  94.9 45.8 %copy-start.3 = (f32[1,1,128,2048]{2,3,1,0:T(8,128)}, f32[1,1,128,2048]{2,3,1,0:T(8,128)S(1)}, u32[]{:S(2)}) copy-start(f32[1,1,128,2048]{2,3,1,0:T(8,128)S(1)} %copy.214) | copy-start | bytes 3145732
  140.7 8.8 %copy-start.1 = (bf16[2048,256]{1,0:T(8,128)(2,1)S(1)}, bf16[2048,256]{1,0:T(8,128)(2,1)}, u32[]{:S(2)}) copy-start(bf16[2048,256]{1,0:T(8,128)(2,1)} %all-gather.9.cloned.1.call-done) | copy-start | bytes 3145732
  151.7 3.3 copy-start.14
  151.7 3.3 copy-start.16
  151.7 3.3 copy-start.31
  151.7 3.3 copy-start.33
  151.7 3.3 copy-start.43
  155.0 4.2 copy-start.18
  171.0 5.8 %copy-start.61 = (bf16[2,1,32]{2,1,0:T(2,128)(2,1)S(1)}, bf16[2,1,32]{2,1,0:T(2,128)(2,1)}, u32[]{:S(2)}) copy-start(bf16[2,1,32]{2,1,0:T(2,128)(2,1)} %all_gather.30) | copy-start | bytes 388
  172.1 51.0 %all-to-all-start.3 = ((bf16[16,8,2048]{2,1,0:T(8,128)(2,1)}), bf16[16,8,2048]{2,1,0:T(8,128)(2,1)}, u32[]{:S(2)}, u32[]{:S(2)}) async-start(bf16[16,8,2048]{2,1,0:T(8,128)(2,1)} %fusion.3), calls=%async_computation.3 | async-start | bytes 1048576 | tf_op jit(solution)/shard_map/all_to_all | solution.py:203
  176.6 26.0 %all-gather.11.cloned.1.call-start = ((), (), s32[]{:S(2)}) async-start(), calls=%async_computation.11 | async-start | bytes 1572864 | tf_op jit(solution)/shard_map/all_gather | solution.py:13
  189.9 5.6 %copy-start.19 = (bf16[1,1,128,2048]{2,3,1,0:T(8,128)(2,1)S(1)}, bf16[1,1,128,2048]{2,3,1,0:T(8,128)(2,1)}, u32[]{:S(2)}) copy-start(bf16[1,1,128,2048]{2,3,1,0:T(8,128)(2,1)} %copy.217) | copy-start | bytes 1572868
  189.9 49.6 %all-reduce.8.cloned.1.call-start = ((), (), s32[]{:S(2)}) async-start(), calls=%async_computation.14 | async-start | bytes 2359296 | tf_op jit(solution)/shard_map/psum | solution.py:231
  195.5 3.8 copy-start.49
  199.3 3.4 copy-start.25
  199.3 3.4 copy-start.62
  203.0 3.6 copy-start.7
  208.9 6.6 %copy-start.26 = (f32[128,128]{1,0:T(8,128)S(1)}, f32[128,128]{1,0:T(8,128)}, u32[]{:S(2)}) copy-start(f32[128,128]{1,0:T(8,128)} %copy-done.25) | copy-start | bytes 196612
  208.9 6.6 %copy-start.28 = (bf16[128,128]{1,0:T(8,128)(2,1)S(1)}, bf16[128,128]{1,0:T(8,128)(2,1)}, u32[]{:S(2)}) copy-start(bf16[128,128]{1,0:T(8,128)(2,1)} %fusion.35) | copy-start | bytes 98308
  208.9 6.8 %copy-start.13 = (f32[2048,256]{1,0:T(8,128)S(1)}, f32[2048,256]{1,0:T(8,128)}, u32[]{:S(2)}) copy-start(f32[2048,256]{1,0:T(8,128)} %convolution_bitcast_fusion) | copy-start | bytes 6291460
  218.1 107.8 %reduce-scatter.10.cloned.1.call-start = ((), (), s32[]{:S(2)}) async-start(), calls=%async_computation.13 | async-start | bytes 2228224
  218.2 3.4 copy-start.2
  218.2 3.4 copy-start.6
  218.2 3.4 copy-start.21
  218.2 3.3 copy-start.35
  231.8 170.5 %reduce-scatter.8.cloned.1.call-start = ((), (), s32[]{:S(2)}) async-start(), calls=%async_computation.10 | async-start | bytes 278528 | tf_op jit(solution)/shard_map/reduce_scatter | solution.py:237
  241.2 241.1 %reduce-scatter.6.cloned.1.call-start = ((), (), s32[]{:S(2)}) async-start(), calls=%async_computation.9 | async-start | bytes 2228224 | tf_op jit(solution)/shard_map/reduce_scatter | solution.py:236
  245.8 8.7 %copy-start.10 = (f32[1,1,128,2048]{2,3,1,0:T(8,128)S(1)}, f32[1,1,128,2048]{2,3,1,0:T(8,128)}, u32[]{:S(2)}) copy-start(f32[1,1,128,2048]{2,3,1,0:T(8,128)} %copy.191) | copy-start | bytes 3145732
  245.8 8.7 %copy-start.39 = (f32[32,64]{1,0:T(8,128)S(1)}, f32[32,64]{1,0:T(8,128)}, u32[]{:S(2)}) copy-start(f32[32,64]{1,0:T(8,128)} %add.246) | copy-start | bytes 24580
  245.8 8.7 %copy-start.41 = (f32[32,64]{1,0:T(8,128)S(1)}, f32[32,64]{1,0:T(8,128)}, u32[]{:S(2)}) copy-start(f32[32,64]{1,0:T(8,128)} %slice.59) | copy-start | bytes 24580
  247.7 25.6 %all-to-all-start.1 = ((bf16[16,8,2048]{2,1,0:T(8,128)(2,1)}), bf16[16,8,2048]{2,1,0:T(8,128)(2,1)S(1)}, u32[]{:S(2)}, u32[]{:S(2)}) async-start(bf16[16,8,2048]{2,1,0:T(8,128)(2,1)} %copy.211), calls=%async_computation.1 | async-start | bytes 1048576 | tf_op jit(solution)/shard_map/all_to_all | solution.py:202
  257.4 4.1 copy-start.59
  257.4 4.1 copy-start.11
  261.5 11.9 %copy-start.12 = (f32[1,1,128,2048]{3,2,1,0:T(8,128)S(1)}, f32[1,1,128,2048]{3,2,1,0:T(8,128)}, u32[]{:S(2)}) copy-start(f32[1,1,128,2048]{3,2,1,0:T(8,128)} %copy.201) | copy-start | bytes 3145732
  262.6 64.3 %copy-start.54 = (f32[256]{0:T(256)S(1)}, f32[256]{0:T(256)}, u32[]{:S(2)}) copy-start(f32[256]{0:T(256)} %get-tuple-element.230) | copy-start | bytes 3076
  (27 other events, 58.6 us)
Sparse Core Ops, SparseCore 0:
  10.7 69.5 all-gather.6
  83.1 54.5 all-gather.8
  140.8 7.8 all-gather.12
  190.0 10.2 all-gather.10
  218.2 21.2 all-reduce.7
  241.7 84.2 reduce-scatter.9
  328.2 74.0 reduce-scatter.7
  404.5 77.7 reduce-scatter.5
where the time goes:
time: 493 us; the launch traced here: 491 us
  waiting for transfers between devices  279 us (57%)
  matrix products  49.4 us (10%)
  blocking collectives  48.2 us (10%)
  local copies, waits for them, and re-layouts  43.1 us (9%)
  other arithmetic  31.3 us (6%)
  starting transfers between devices  24 us (5%)
  between operations  15.8 us (3%)
    reduce_scatter x1, waiting for transfers between devices, per_device(): lax.psum_scatter(proj_sum, 'frame', scatter_dimension=0, tiled=True)  78.7 us
    reduce_scatter x1, waiting for transfers between devices, per_device(): lax.psum_scatter(step_sum, 'frame', scatter_dimension=0, tiled=True)  74.5 us
    unnamed x9, waiting for transfers between devices  51.6 us
    all_gather x1, waiting for transfers between devices, per_device(): lax.all_gather(proj_weight, 'frame', axis=0, tiled=True)  42.8 us
    all_gather x1, blocking collectives, per_device(): lax.all_gather(step_weight, 'frame', axis=0, tiled=True)  42 us
    dot_general x6, matrix products, block_parts(): jnp.einsum('shtu,suhp->sthp', weights, inputs, preferred_element_type=jnp...  17 us
    all_gather x1, waiting for transfers between devices, per_device(): mod_full = lax.all_gather(mod_weight, 'frame', axis=1, tiled=True)  12.4 us
    all_to_all x1, waiting for transfers between devices, per_device(): lax.all_to_all(time_low, 'frame', split_axis=0, concat_axis=0, tiled=True)  10.8 us
  transfers between devices with their start and end apart: 12, of which 7 were waited for; matrix products, arithmetic and copies ran while one was open for 25% of the time, Pallas kernels for 0%

commit v1 on v0

--- a/solution.py
+++ b/solution.py
@@ -5,6 +5,24 @@
 from jax.sharding import PartitionSpec as P
 
 norm_eps = 1e-05
+
+
+def ring_gather(value, axis, dim):
+    ways, here, hop = (lax.axis_size(axis), lax.axis_index(axis), value.shape[dim])
+    shape = [n * ways if d == dim else n for d, n in enumerate(value.shape)]
+    full = lax.dynamic_update_slice_in_dim(
+        jnp.zeros(shape, value.dtype), value, here * hop, axis=dim
+    )
+    going_up = going_down = value
+    for far in range(1, ways // 2 + 1):
+        going_up = lax.ppermute(going_up, axis, [(d, (d + 1) % ways) for d in range(ways)])
+        full = lax.dynamic_update_slice_in_dim(full, going_up, (here - far) % ways * hop, axis=dim)
+        if 2 * far < ways:
+            going_down = lax.ppermute(going_down, axis, [(d, (d - 1) % ways) for d in range(ways)])
+            full = lax.dynamic_update_slice_in_dim(
+                full, going_down, (here + far) % ways * hop, axis=dim
+            )
+    return full
 
 
 def prefix(array, axis, join, neutral):
@@ -137,7 +155,7 @@
     factor = (frame_count * row_count * band_len) ** (-0.5)
     activated = time_embed(timestep, mod_weight.shape[0]).astype(jnp.bfloat16)
     proj_full, step_full = (
-        lax.all_gather(proj_weight, "frame", axis=0, tiled=True),
+        ring_gather(proj_weight, "frame", 0),
         lax.all_gather(step_weight, "frame", axis=0, tiled=True),
     )
     mod_full = lax.all_gather(mod_weight, "frame", axis=1, tiled=True)

time: 493 us -> 509 us (1.032)
  starting transfers between devices: 24 us -> 63.3 us
  waiting for transfers between devices: 279 us -> 251 us
  local copies, waits for them, and re-layouts: 43.1 us -> 49.9 us
    all_gather x1 -> x0, waiting for transfers between devices: 42.8 us -> none  [per_device(): lax.all_gather(proj_weight, 'frame', axis=0, tiled=True)]
    ppermute x0 -> x15, starting transfers between devices: none -> 38.2 us  [the longest x7 36.1 us: ring_gather(): lax.ppermute(going_down, axis, [(d, (d - 1) % ways) for d in range(ways)])]
    ppermute x0 -> x15, waiting for transfers between devices: none -> 26.1 us  [the longest x8 16.1 us: ring_gather(): lax.ppermute(going_up, axis, [(d, (d + 1) % ways) for d in range(ways)])]
    all_gather x1, waiting for transfers between devices: 12.4 us -> 0.01 us  [per_device(): mod_full = lax.all_gather(mod_weight, 'frame', axis=1, tiled=True)]
    unnamed x9 -> x8, waiting for transfers between devices: 51.6 us -> 51.6 us
  transfers between devices with their start and end apart: 12 -> 26, of which waited for: 7 -> 14; matrix products, arithmetic and copies ran while one was open for 25% -> 24% of each run, Pallas kernels for 0% -> 0%
where the time goes in v1:
time: 509 us; the launch traced here: 507 us
  waiting for transfers between devices  251 us (49%)
  starting transfers between devices  63.3 us (12%)
  local copies, waits for them, and re-layouts  49.9 us (10%)
  matrix products  48.6 us (10%)
  blocking collectives  47.5 us (9%)
  other arithmetic  30.3 us (6%)
  between operations  16.1 us (3%)
    reduce_scatter x1, waiting for transfers between devices, per_device(): lax.psum_scatter(proj_sum, 'frame', scatter_dimension=0, tiled=True)  78.7 us
    reduce_scatter x1, waiting for transfers between devices, per_device(): lax.psum_scatter(step_sum, 'frame', scatter_dimension=0, tiled=True)  74.5 us
    unnamed x8, waiting for transfers between devices  51.6 us
    all_gather x1, blocking collectives, per_device(): lax.all_gather(step_weight, 'frame', axis=0, tiled=True)  42.4 us
    ppermute x7, starting transfers between devices, ring_gather(): lax.ppermute(going_down, axis, [(d, (d - 1) % ways) for d in range(ways)])  36.1 us
    dot_general x6, matrix products, block_parts(): jnp.einsum('shtu,suhp->sthp', weights, inputs, preferred_element_type=jnp...  19.1 us
    ppermute x8, waiting for transfers between devices, ring_gather(): lax.ppermute(going_up, axis, [(d, (d + 1) % ways) for d in range(ways)])  16.1 us
    all_to_all x1, waiting for transfers between devices, per_device(): lax.all_to_all(time_low, 'frame', split_axis=0, concat_axis=0, tiled=True)  10.7 us
  transfers between devices with their start and end apart: 26, of which 14 were waited for; matrix products, arithmetic and copies ran while one was open for 24% of the time, Pallas kernels for 0%

profile of v1, /device:TPU:0, one launch (start us, length us, event | category | flops | bytes accessed | tf_op | source)
XLA Modules:
  0.0 506.7 jit_solution(9540948758815477897)
XLA Ops:
  7.9 7.0 %collective-permute-start.1 = (bf16[128,256]{1,0:T(8,128)(2,1)}, bf16[128,256]{1,0:T(8,128)(2,1)S(1)}, u32[]{:S(2)}, u32[]{:S(2)}) collective-permute-start(bf16[128,256]{1,0:T(8,128)(2,1)} %param.20), channel_id=1, source_target_pairs={{0,30},{2,0},{4,2},{6,4},{8,6},{10,8},{12,10},{14,12},{16,14},{18,... | collective-permute-start | bytes 196616 | tf_op jit(solution)/shard_map/ppermute | solution.py:21
  14.9 7.0 %all-to-all-start.2 = ((bf16[16,8,2048]{2,1,0:T(8,128)(2,1)}), bf16[16,8,2048]{2,1,0:T(8,128)(2,1)S(1)}, u32[]{:S(2)}, u32[]{:S(2)}) async-start(bf16[16,8,2048]{2,1,0:T(8,128)(2,1)} %bitcast.449), calls=%async_computation.2 | async-start | bytes 1048576 | tf_op jit(solution)/shard_map/all_to_all | solution.py:186
  27.6 42.4 %all_gather.25 = bf16[2048,32]{0,1:T(8,128)(2,1)S(1)} all-gather(bf16[128,32]{0,1:T(8,128)(2,1)S(1)} %copy-done.45), channel_id=1, replica_groups=mesh['frame'=16,'row'=2] {'frame'}, dimensions={0}, use_global_device_ids=true | all-gather | bytes 139264 | tf_op jit(solution)/shard_map/all_gather | solution.py:159
  70.0 2.0 collective-permute-start.2
  72.0 2.2 collective-permute-done.3
  74.2 5.1 collective-permute-start.5
  79.3 2.2 collective-permute-done.5
  81.5 6.1 %collective-permute-start.7 = (bf16[128,256]{1,0:T(8,128)(2,1)S(1)}, bf16[128,256]{1,0:T(8,128)(2,1)S(1)}, u32[]{:S(2)}, u32[]{:S(2)}) collective-permute-start(bf16[128,256]{1,0:T(8,128)(2,1)S(1)} %collective-permute-done.5), channel_id=1, source_target_pairs={{0,30},{2,0},{4,2},{6,4},{8,6},{10,8},{12,10},{14,12},{16,14},{18,... | collective-permute-start | bytes 196616 | tf_op jit(solution)/shard_map/ppermute | solution.py:21
  89.5 6.1 %collective-permute-start.9 = (bf16[128,256]{1,0:T(8,128)(2,1)S(1)}, bf16[128,256]{1,0:T(8,128)(2,1)S(1)}, u32[]{:S(2)}, u32[]{:S(2)}) collective-permute-start(bf16[128,256]{1,0:T(8,128)(2,1)S(1)} %collective-permute-done.7), channel_id=1, source_target_pairs={{0,30},{2,0},{4,2},{6,4},{8,6},{10,8},{12,10},{14,12},{16,14},{18,... | collective-permute-start | bytes 196616 | tf_op jit(solution)/shard_map/ppermute | solution.py:21
  97.5 6.0 %collective-permute-start.11 = (bf16[128,256]{1,0:T(8,128)(2,1)S(1)}, bf16[128,256]{1,0:T(8,128)(2,1)S(1)}, u32[]{:S(2)}, u32[]{:S(2)}) collective-permute-start(bf16[128,256]{1,0:T(8,128)(2,1)S(1)} %collective-permute-done.9), channel_id=1, source_target_pairs={{0,30},{2,0},{4,2},{6,4},{8,6},{10,8},{12,10},{14,12},{16,14},{18,... | collective-permute-start | bytes 196616 | tf_op jit(solution)/shard_map/ppermute | solution.py:21
  105.3 6.0 %collective-permute-start.13 = (bf16[128,256]{1,0:T(8,128)(2,1)S(1)}, bf16[128,256]{1,0:T(8,128)(2,1)S(1)}, u32[]{:S(2)}, u32[]{:S(2)}) collective-permute-start(bf16[128,256]{1,0:T(8,128)(2,1)S(1)} %collective-permute-done.11), channel_id=1, source_target_pairs={{0,30},{2,0},{4,2},{6,4},{8,6},{10,8},{12,10},{14,12},{16,14},{18,... | collective-permute-start | bytes 196616 | tf_op jit(solution)/shard_map/ppermute | solution.py:21
  111.8 7.8 %collective-permute-done.12 = bf16[128,256]{1,0:T(8,128)(2,1)S(1)} collective-permute-done((bf16[128,256]{1,0:T(8,128)(2,1)S(1)}, bf16[128,256]{1,0:T(8,128)(2,1)S(1)}, u32[]{:S(2)}, u32[]{:S(2)}) %collective-permute-start.12) | collective-permute-done | bytes 65568 | tf_op jit(solution)/shard_map/ppermute | solution.py:18
  119.6 7.8 %collective-permute-done.14 = bf16[128,256]{1,0:T(8,128)(2,1)S(1)} collective-permute-done((bf16[128,256]{1,0:T(8,128)(2,1)S(1)}, bf16[128,256]{1,0:T(8,128)(2,1)S(1)}, u32[]{:S(2)}, u32[]{:S(2)}) %collective-permute-start.14) | collective-permute-done | bytes 65568 | tf_op jit(solution)/shard_map/ppermute | solution.py:18
  127.5 2.1 reshape.933
  129.5 2.0 fusion.186
  135.9 3.6 all-to-all-start
  140.8 2.5 copy.213
  143.3 2.8 convert_multiply_fusion
  146.1 2.6 copy.223
  148.8 2.5 copy.214
  155.7 2.0 reshape.936
  158.2 4.1 convert_bitcast_fusion
  162.3 4.5 fusion.28
  168.1 3.6 copy.231
  171.7 2.8 reshape.922
  177.4 6.8 %all-to-all-start.3 = ((bf16[16,8,2048]{2,1,0:T(8,128)(2,1)}), bf16[16,8,2048]{2,1,0:T(8,128)(2,1)}, u32[]{:S(2)}, u32[]{:S(2)}) async-start(bf16[16,8,2048]{2,1,0:T(8,128)(2,1)} %fusion.5), calls=%async_computation.3 | async-start | bytes 1048576 | tf_op jit(solution)/shard_map/all_to_all | solution.py:221
  185.8 2.5 multiply_reduce_fusion.2
  190.8 2.5 copy.197
  193.4 2.3 fusion.52
  198.4 2.7 convolution_bitcast_fusion
  204.5 4.1 fusion.26
  213.2 2.4 fusion.37
  215.6 2.3 multiply_reduce_fusion.1
  225.0 2.6 reduce_window_sum.49
  229.2 2.0 fusion.6
  232.2 2.4 fusion
  234.7 2.3 fusion.34
  238.3 3.0 fusion.72
  241.3 3.4 psum.23
  246.6 9.2 %all-reduce.8.cloned.1.call-done = (bf16[2048,256]{1,0:T(8,128)(2,1)}, bf16[2048,32]{0,1:T(8,128)(2,1)}) async-done(((bf16[2048,256]{1,0:T(8,128)(2,1)}, bf16[2048,32]{0,1:T(8,128)(2,1)}), (bf16[2048,256]{1,0:T(8,128)(2,1)}, bf16[2048,32]{0,1:T(8,128)(2,1)})) %all-reduce.8.cloned.1.call-update) | async-done | bytes 1179664 | tf_op jit(solution)/shard_map/psum | solution.py:249
  257.7 2.8 convert_element_type.533
  264.2 6.8 %all-to-all-start.1 = ((bf16[16,8,2048]{2,1,0:T(8,128)(2,1)}), bf16[16,8,2048]{2,1,0:T(8,128)(2,1)S(1)}, u32[]{:S(2)}, u32[]{:S(2)}) async-start(bf16[16,8,2048]{2,1,0:T(8,128)(2,1)} %copy.211), calls=%async_computation.1 | async-start | bytes 1048576 | tf_op jit(solution)/shard_map/all_to_all | solution.py:220
  271.0 2.8 fusion.82
  276.8 2.4 fusion.83
  279.2 10.7 %all-to-all-done.1 = bf16[16,8,2048]{2,1,0:T(8,128)(2,1)S(1)} async-done(((bf16[16,8,2048]{2,1,0:T(8,128)(2,1)}), bf16[16,8,2048]{2,1,0:T(8,128)(2,1)S(1)}, u32[]{:S(2)}, u32[]{:S(2)}) %all-to-all-start.1) | async-done | bytes 524320 | tf_op jit(solution)/shard_map/all_to_all | solution.py:220
  291.1 50.8 %reduce-scatter.10.cloned.1.call-done = f32[256,1]{1,0:T(8,128)} async-done(((f32[4096,1]{1,0:T(8,128)}), f32[256,1]{1,0:T(8,128)}) %reduce-scatter.10.cloned.1.call-update) | async-done | bytes 1040
  343.7 74.5 %reduce-scatter.8.cloned.1.call-done = f32[128,32]{0,1:T(8,128)} async-done(((f32[2048,32]{0,1:T(8,128)}), f32[128,32]{0,1:T(8,128)}) %reduce-scatter.8.cloned.1.call-update) | async-done | bytes 16400 | tf_op jit(solution)/shard_map/reduce_scatter | solution.py:255
  419.5 78.7 %reduce-scatter.6.cloned.1.call-done = f32[128,256]{1,0:T(8,128)} async-done(((f32[2048,256]{1,0:T(8,128)}), f32[128,256]{1,0:T(8,128)}) %reduce-scatter.6.cloned.1.call-update) | async-done | bytes 131088 | tf_op jit(solution)/shard_map/reduce_scatter | solution.py:254
  (261 shorter events, 69.3 us)
Async XLA Ops:
  7.2 17.0 %copy-start.35 = (bf16[128,256]{1,0:T(8,128)(2,1)S(1)}, bf16[128,256]{1,0:T(8,128)(2,1)}, u32[]{:S(2)}) copy-start(bf16[128,256]{1,0:T(8,128)(2,1)} %param.20) | copy-start | bytes 196612
  7.2 17.3 %copy-start.5 = (bf16[1,1,128,2048]{3,2,1,0:T(8,128)(2,1)S(1)}, bf16[1,1,128,2048]{3,2,1,0:T(8,128)(2,1)}, u32[]{:S(2)}) copy-start(bf16[1,1,128,2048]{3,2,1,0:T(8,128)(2,1)} %param.17) | copy-start | bytes 1572868
  7.2 17.1 %copy-start = (bf16[1,1,128,2048]{3,2,1,0:T(8,128)(2,1)S(1)}, bf16[1,1,128,2048]{3,2,1,0:T(8,128)(2,1)}, u32[]{:S(2)}) copy-start(bf16[1,1,128,2048]{3,2,1,0:T(8,128)(2,1)} %param.16) | copy-start | bytes 1572868
  7.2 122.3 %all-gather.6.cloned.1.call-start = ((), (), s32[]{:S(2)}) async-start(), calls=%async_computation.7 | async-start | bytes 2228224 | tf_op jit(solution)/shard_map/all_gather | solution.py:161
  7.9 62.0 %collective-permute-start.1 = (bf16[128,256]{1,0:T(8,128)(2,1)}, bf16[128,256]{1,0:T(8,128)(2,1)S(1)}, u32[]{:S(2)}, u32[]{:S(2)}) collective-permute-start(bf16[128,256]{1,0:T(8,128)(2,1)} %param.20), channel_id=1, source_target_pairs={{0,30},{2,0},{4,2},{6,4},{8,6},{10,8},{12,10},{14,12},{16,14},{18,... | collective-permute-start | bytes 196616 | tf_op jit(solution)/shard_map/ppermute | solution.py:21
  14.9 55.0 %collective-permute-start = (bf16[128,256]{1,0:T(8,128)(2,1)}, bf16[128,256]{1,0:T(8,128)(2,1)S(1)}, u32[]{:S(2)}, u32[]{:S(2)}) collective-permute-start(bf16[128,256]{1,0:T(8,128)(2,1)} %param.20), channel_id=1, source_target_pairs={{0,2},{2,4},{4,6},{6,8},{8,10},{10,12},{12,14},{14,16},{16,18},{18... | collective-permute-start | bytes 196616 | tf_op jit(solution)/shard_map/ppermute | solution.py:18
  14.9 112.5 %all-to-all-start.2 = ((bf16[16,8,2048]{2,1,0:T(8,128)(2,1)}), bf16[16,8,2048]{2,1,0:T(8,128)(2,1)S(1)}, u32[]{:S(2)}, u32[]{:S(2)}) async-start(bf16[16,8,2048]{2,1,0:T(8,128)(2,1)} %bitcast.449), calls=%async_computation.2 | async-start | bytes 1048576 | tf_op jit(solution)/shard_map/all_to_all | solution.py:186
  23.5 134.7 %copy-start.51 = (pred[16,16]{1,0:T(8,128)(4,1)}, pred[16,16]{1,0:T(8,128)(4,1)S(1)}, u32[]{:S(2)}) copy-start(pred[16,16]{1,0:T(8,128)(4,1)S(1)} %iota_compare_fusion.1) | copy-start | bytes 772
  24.5 168.9 %copy-start.39 = (f32[128]{0:T(128)}, f32[128]{0:T(128)S(1)}, u32[]{:S(2)}) copy-start(f32[128]{0:T(128)S(1)} %fusion.162) | copy-start | bytes 1540
  70.0 4.3 collective-permute-start.3
  70.0 9.3 %collective-permute-start.2 = (bf16[128,256]{1,0:T(8,128)(2,1)S(1)}, bf16[128,256]{1,0:T(8,128)(2,1)S(1)}, u32[]{:S(2)}, u32[]{:S(2)}) collective-permute-start(bf16[128,256]{1,0:T(8,128)(2,1)S(1)} %collective-permute-done), channel_id=1, source_target_pairs={{0,2},{2,4},{4,6},{6,8},{8,10},{10,12},{12,14},{14,16},{16,18},{18... | collective-permute-start | bytes 196616 | tf_op jit(solution)/shard_map/ppermute | solution.py:18
  74.2 7.3 %collective-permute-start.5 = (bf16[128,256]{1,0:T(8,128)(2,1)S(1)}, bf16[128,256]{1,0:T(8,128)(2,1)S(1)}, u32[]{:S(2)}, u32[]{:S(2)}) collective-permute-start(bf16[128,256]{1,0:T(8,128)(2,1)S(1)} %collective-permute-done.3), channel_id=1, source_target_pairs={{0,30},{2,0},{4,2},{6,4},{8,6},{10,8},{12,10},{14,12},{16,14},{18,... | collective-permute-start | bytes 196616 | tf_op jit(solution)/shard_map/ppermute | solution.py:21
  79.3 8.3 %collective-permute-start.4 = (bf16[128,256]{1,0:T(8,128)(2,1)S(1)}, bf16[128,256]{1,0:T(8,128)(2,1)S(1)}, u32[]{:S(2)}, u32[]{:S(2)}) collective-permute-start(bf16[128,256]{1,0:T(8,128)(2,1)S(1)} %collective-permute-done.2), channel_id=1, source_target_pairs={{0,2},{2,4},{4,6},{6,8},{8,10},{10,12},{12,14},{14,16},{16,18},{18... | collective-permute-start | bytes 196616 | tf_op jit(solution)/shard_map/ppermute | solution.py:18
  81.5 8.0 %collective-permute-start.7 = (bf16[128,256]{1,0:T(8,128)(2,1)S(1)}, bf16[128,256]{1,0:T(8,128)(2,1)S(1)}, u32[]{:S(2)}, u32[]{:S(2)}) collective-permute-start(bf16[128,256]{1,0:T(8,128)(2,1)S(1)} %collective-permute-done.5), channel_id=1, source_target_pairs={{0,30},{2,0},{4,2},{6,4},{8,6},{10,8},{12,10},{14,12},{16,14},{18,... | collective-permute-start | bytes 196616 | tf_op jit(solution)/shard_map/ppermute | solution.py:21
  87.6 8.0 %collective-permute-start.6 = (bf16[128,256]{1,0:T(8,128)(2,1)S(1)}, bf16[128,256]{1,0:T(8,128)(2,1)S(1)}, u32[]{:S(2)}, u32[]{:S(2)}) collective-permute-start(bf16[128,256]{1,0:T(8,128)(2,1)S(1)} %collective-permute-done.4), channel_id=1, source_target_pairs={{0,2},{2,4},{4,6},{6,8},{8,10},{10,12},{12,14},{14,16},{16,18},{18... | collective-permute-start | bytes 196616 | tf_op jit(solution)/shard_map/ppermute | solution.py:18
  89.5 8.0 %collective-permute-start.9 = (bf16[128,256]{1,0:T(8,128)(2,1)S(1)}, bf16[128,256]{1,0:T(8,128)(2,1)S(1)}, u32[]{:S(2)}, u32[]{:S(2)}) collective-permute-start(bf16[128,256]{1,0:T(8,128)(2,1)S(1)} %collective-permute-done.7), channel_id=1, source_target_pairs={{0,30},{2,0},{4,2},{6,4},{8,6},{10,8},{12,10},{14,12},{16,14},{18,... | collective-permute-start | bytes 196616 | tf_op jit(solution)/shard_map/ppermute | solution.py:21
  95.6 7.9 %collective-permute-start.8 = (bf16[128,256]{1,0:T(8,128)(2,1)S(1)}, bf16[128,256]{1,0:T(8,128)(2,1)S(1)}, u32[]{:S(2)}, u32[]{:S(2)}) collective-permute-start(bf16[128,256]{1,0:T(8,128)(2,1)S(1)} %collective-permute-done.6), channel_id=1, source_target_pairs={{0,2},{2,4},{4,6},{6,8},{8,10},{10,12},{12,14},{14,16},{16,18},{18... | collective-permute-start | bytes 196616 | tf_op jit(solution)/shard_map/ppermute | solution.py:18
  97.5 7.9 %collective-permute-start.11 = (bf16[128,256]{1,0:T(8,128)(2,1)S(1)}, bf16[128,256]{1,0:T(8,128)(2,1)S(1)}, u32[]{:S(2)}, u32[]{:S(2)}) collective-permute-start(bf16[128,256]{1,0:T(8,128)(2,1)S(1)} %collective-permute-done.9), channel_id=1, source_target_pairs={{0,30},{2,0},{4,2},{6,4},{8,6},{10,8},{12,10},{14,12},{16,14},{18,... | collective-permute-start | bytes 196616 | tf_op jit(solution)/shard_map/ppermute | solution.py:21
  103.4 8.3 %collective-permute-start.10 = (bf16[128,256]{1,0:T(8,128)(2,1)S(1)}, bf16[128,256]{1,0:T(8,128)(2,1)S(1)}, u32[]{:S(2)}, u32[]{:S(2)}) collective-permute-start(bf16[128,256]{1,0:T(8,128)(2,1)S(1)} %collective-permute-done.8), channel_id=1, source_target_pairs={{0,2},{2,4},{4,6},{6,8},{8,10},{10,12},{12,14},{14,16},{16,18},{18... | collective-permute-start | bytes 196616 | tf_op jit(solution)/shard_map/ppermute | solution.py:18
  105.3 14.3 %collective-permute-start.13 = (bf16[128,256]{1,0:T(8,128)(2,1)S(1)}, bf16[128,256]{1,0:T(8,128)(2,1)S(1)}, u32[]{:S(2)}, u32[]{:S(2)}) collective-permute-start(bf16[128,256]{1,0:T(8,128)(2,1)S(1)} %collective-permute-done.11), channel_id=1, source_target_pairs={{0,30},{2,0},{4,2},{6,4},{8,6},{10,8},{12,10},{14,12},{16,14},{18,... | collective-permute-start | bytes 196616 | tf_op jit(solution)/shard_map/ppermute | solution.py:21
  111.7 7.9 %collective-permute-start.12 = (bf16[128,256]{1,0:T(8,128)(2,1)S(1)}, bf16[128,256]{1,0:T(8,128)(2,1)S(1)}, u32[]{:S(2)}, u32[]{:S(2)}) collective-permute-start(bf16[128,256]{1,0:T(8,128)(2,1)S(1)} %collective-permute-done.10), channel_id=1, source_target_pairs={{0,2},{2,4},{4,6},{6,8},{8,10},{10,12},{12,14},{14,16},{16,18},{18... | collective-permute-start | bytes 196616 | tf_op jit(solution)/shard_map/ppermute | solution.py:18
  111.8 19.9 %copy-start.46 = (f32[32]{0:T(128)S(1)}, f32[32]{0:T(128)}, u32[]{:S(2)}) copy-start(f32[32]{0:T(128)} %param.22) | copy-start | bytes 388
  119.6 7.9 %collective-permute-start.14 = (bf16[128,256]{1,0:T(8,128)(2,1)S(1)}, bf16[128,256]{1,0:T(8,128)(2,1)S(1)}, u32[]{:S(2)}, u32[]{:S(2)}) collective-permute-start(bf16[128,256]{1,0:T(8,128)(2,1)S(1)} %collective-permute-done.12), channel_id=1, source_target_pairs={{0,2},{2,4},{4,6},{6,8},{8,10},{10,12},{12,14},{14,16},{16,18},{18... | collective-permute-start | bytes 196616 | tf_op jit(solution)/shard_map/ppermute | solution.py:18
  127.5 47.6 %copy-start.1 = (bf16[2048,256]{1,0:T(8,128)(2,1)}, bf16[2048,256]{1,0:T(8,128)(2,1)S(1)}, u32[]{:S(2)}) copy-start(bf16[2048,256]{1,0:T(8,128)(2,1)S(1)} %constant_dynamic-update-slice_fusion) | copy-start | bytes 3145732
  131.6 54.2 %copy-start.31 = (f32[32,64]{1,0:T(8,128)}, f32[32,64]{1,0:T(8,128)S(1)}, u32[]{:S(2)}) copy-start(f32[32,64]{1,0:T(8,128)S(1)} %slice.59) | copy-start | bytes 24580
  131.7 54.1 %copy-start.33 = (f32[32,64]{1,0:T(8,128)}, f32[32,64]{1,0:T(8,128)S(1)}, u32[]{:S(2)}) copy-start(f32[32,64]{1,0:T(8,128)S(1)} %add.369) | copy-start | bytes 24580
  132.3 56.1 %copy-start.50 = (f32[32]{0:T(128)}, f32[32]{0:T(128)S(1)}, u32[]{:S(2)}) copy-start(f32[32]{0:T(128)S(1)} %get-tuple-element.241) | copy-start | bytes 388
  135.9 19.0 %all-to-all-start = ((bf16[16,8,2048]{2,1,0:T(8,128)(2,1)}), bf16[16,8,2048]{2,1,0:T(8,128)(2,1)S(1)}, u32[]{:S(2)}, u32[]{:S(2)}) async-start(bf16[16,8,2048]{2,1,0:T(8,128)(2,1)} %fusion.64), calls=%async_computation | async-start | bytes 1048576 | tf_op jit(solution)/shard_map/all_to_all | solution.py:185
  139.5 44.8 %all-gather.10.cloned.1.call-start = ((), (), s32[]{:S(2)}) async-start(), calls=%async_computation.11 | async-start | bytes 1572864 | tf_op jit(solution)/shard_map/all_gather | solution.py:53
  155.5 6.8 %copy-start.21 = (f32[8,32,16]{2,1,0:T(8,128)}, f32[8,32,16]{2,1,0:T(8,128)S(1)}, u32[]{:S(2)}) copy-start(f32[8,32,16]{2,1,0:T(8,128)S(1)} %copy.208) | copy-start | bytes 49156
  158.2 4.1 copy-start.37
  158.2 4.1 copy-start.12
  158.2 4.1 copy-start.14
  175.8 8.6 %copy-start.56 = (bf16[2,1,32]{2,1,0:T(2,128)(2,1)S(1)}, bf16[2,1,32]{2,1,0:T(2,128)(2,1)}, u32[]{:S(2)}) copy-start(bf16[2,1,32]{2,1,0:T(2,128)(2,1)} %all_gather.26) | copy-start | bytes 388
  177.4 60.9 %all-to-all-start.3 = ((bf16[16,8,2048]{2,1,0:T(8,128)(2,1)}), bf16[16,8,2048]{2,1,0:T(8,128)(2,1)}, u32[]{:S(2)}, u32[]{:S(2)}) async-start(bf16[16,8,2048]{2,1,0:T(8,128)(2,1)} %fusion.5), calls=%async_computation.3 | async-start | bytes 1048576 | tf_op jit(solution)/shard_map/all_to_all | solution.py:221
  184.2 27.6 %all-gather.8.cloned.1.call-start = ((), (), s32[]{:S(2)}) async-start(), calls=%async_computation.10 | async-start | bytes 1572864 | tf_op jit(solution)/shard_map/all_gather | solution.py:31
  198.1 57.6 %all-reduce.8.cloned.1.call-start = ((), (), s32[]{:S(2)}) async-start(), calls=%async_computation.13 | async-start | bytes 2359296 | tf_op jit(solution)/shard_map/psum | solution.py:249
  202.9 5.6 %copy-start.42 = (f32[32,128]{1,0:T(8,128)}, f32[32,128]{1,0:T(8,128)S(1)}, u32[]{:S(2)}) copy-start(f32[32,128]{1,0:T(8,128)S(1)} %copy.195) | copy-start | bytes 49156
  218.0 14.1 %copy-start.11 = (f32[2048,256]{1,0:T(8,128)S(1)}, f32[2048,256]{1,0:T(8,128)}, u32[]{:S(2)}) copy-start(f32[2048,256]{1,0:T(8,128)} %convolution_bitcast_fusion) | copy-start | bytes 6291460
  234.6 107.4 %reduce-scatter.10.cloned.1.call-start = ((), (), s32[]{:S(2)}) async-start(), calls=%async_computation.12 | async-start | bytes 2228224
  246.5 171.7 %reduce-scatter.8.cloned.1.call-start = ((), (), s32[]{:S(2)}) async-start(), calls=%async_computation.9 | async-start | bytes 278528 | tf_op jit(solution)/shard_map/reduce_scatter | solution.py:255
  257.4 240.9 %reduce-scatter.6.cloned.1.call-start = ((), (), s32[]{:S(2)}) async-start(), calls=%async_computation.8 | async-start | bytes 2228224 | tf_op jit(solution)/shard_map/reduce_scatter | solution.py:254
  262.2 8.7 %copy-start.9 = (f32[1,1,128,2048]{2,3,1,0:T(8,128)S(1)}, f32[1,1,128,2048]{2,3,1,0:T(8,128)}, u32[]{:S(2)}) copy-start(f32[1,1,128,2048]{2,3,1,0:T(8,128)} %copy.191) | copy-start | bytes 3145732
  262.2 8.7 %copy-start.32 = (f32[32,64]{1,0:T(8,128)S(1)}, f32[32,64]{1,0:T(8,128)}, u32[]{:S(2)}) copy-start(f32[32,64]{1,0:T(8,128)} %copy-done.31) | copy-start | bytes 24580
  262.2 8.7 %copy-start.34 = (f32[32,64]{1,0:T(8,128)S(1)}, f32[32,64]{1,0:T(8,128)}, u32[]{:S(2)}) copy-start(f32[32,64]{1,0:T(8,128)} %copy-done.33) | copy-start | bytes 24580
  264.2 25.8 %all-to-all-start.1 = ((bf16[16,8,2048]{2,1,0:T(8,128)(2,1)}), bf16[16,8,2048]{2,1,0:T(8,128)(2,1)S(1)}, u32[]{:S(2)}, u32[]{:S(2)}) async-start(bf16[16,8,2048]{2,1,0:T(8,128)(2,1)} %copy.211), calls=%async_computation.1 | async-start | bytes 1048576 | tf_op jit(solution)/shard_map/all_to_all | solution.py:220
  276.8 13.1 %copy-start.10 = (f32[1,1,128,2048]{3,2,1,0:T(8,128)S(1)}, f32[1,1,128,2048]{3,2,1,0:T(8,128)}, u32[]{:S(2)}) copy-start(f32[1,1,128,2048]{3,2,1,0:T(8,128)} %copy.202) | copy-start | bytes 3145732
  279.2 63.7 %copy-start.47 = (f32[256]{0:T(256)S(1)}, f32[256]{0:T(256)}, u32[]{:S(2)}) copy-start(f32[256]{0:T(256)} %get-tuple-element.230) | copy-start | bytes 3076
  (35 other events, 84.9 us)
Sparse Core Ops, SparseCore 0:
  10.7 73.3 all-gather.5
  154.1 10.2 all-gather.9
  198.2 10.2 all-gather.7
  234.7 20.9 all-reduce.7
  257.8 84.0 reduce-scatter.9
  344.0 74.1 reduce-scatter.7
  420.5 77.7 reduce-scatter.5
